TPU v7x, 32 devices: a whole 2x2x4 slice. The times are simulated.
32 devices in a mesh: row: 4 (over z), col: 8 (over y, x, core).
Axes of the slice: x: 2, y: 2, z: 4, core: 2. Of those that a mesh axis runs over, the one named last changes fastest.
Arguments:
- solution: float32 [8, 8, 4, 8, 256], P(None, None, 'row', 'col'), may hold values from -6 to 6
- residual: float32 [8, 8, 4, 8, 256], P(None, None, 'row', 'col'), may hold values from -120 to 120
- direction: float32 [8, 8, 4, 8, 256], P(None, None, 'row', 'col'), may hold values from -120 to 120
- noise_var: float32 [8, 4, 8, 256], P(None, 'row', 'col'), may hold values from 2 to 4
- coords: float32 [3, 8, 4, 8, 256], P(None, None, 'row', 'col'), may hold values from 0 to 128
- tile_pairs: int32 [2, 4, 8, 64], P(None, 'row', 'col'), may hold values from 0 to 63, as said below
- tile_count: int32 [4, 8], P('row', 'col'), may hold values from 1 to 64, as said below
Outputs:
- new_solution: float32 [8, 8, 4, 8, 256], P(None, None, 'row', 'col')
- new_residual: float32 [8, 8, 4, 8, 256], P(None, None, 'row', 'col')
- new_direction: float32 [8, 8, 4, 8, 256], P(None, None, 'row', 'col')
Inputs may be any that keep to these rules, and one draw needn't show every extreme that they name: `tile_pairs`: entry [0, g, h, s] is one of the 64 row tiles of cell (g, h) and entry [1, g, h, s] one of its 32 column tiles; the first tile_count[g, h] pairs of a cell are distinct, and the mirror pair of each of them is live in the cell that holds it, so the kernel that the lists define is symmetric. `tile_count`: some cell holds exactly 64 live pairs.
All inputs are finite; a program needn't handle non-finite values.
Results may differ from a plain program's by a relative error of at most 0.0003.
Values sent between devices are 32-bit elements; how exact they have to be, the bound alone decides.
No kernel may reach another device: no remote copies, remote signals or barrier semaphores. Data moves between devices by JAX's collectives and lax.ppermute only.
A program may use at most 64 MiB of HBM per device.

v0:
```python
import jax
import jax.numpy as jnp
from jax import lax
from jax.sharding import PartitionSpec as P

EPS = 1e-06
KERNEL_SCALE = 0.125
HIGHEST = lax.Precision.HIGHEST


def wendland(target_pts, source_pts):
    delta_x = target_pts[0][:, None] - source_pts[0][None, :]
    delta_y = target_pts[1][:, None] - source_pts[1][None, :]
    delta_z = target_pts[2][:, None] - source_pts[2][None, :]
    distance = jnp.sqrt(delta_x * delta_x + delta_y * delta_y + delta_z * delta_z)
    reach_left = jnp.maximum(1.0 - distance, 0.0)
    squared = reach_left * reach_left
    return squared * squared * (4.0 * distance + 1.0)


def run_tiles(
    partial_value, start_slot, stop_slot, target_ids, source_ids, target_pts, source_pts, source_dir
):

    def add_tile(pair_slot, totals):
        target = target_ids[pair_slot]
        source = source_ids[pair_slot]
        kernel_block = wendland(
            lax.dynamic_index_in_dim(target_pts, target, 1, False),
            lax.dynamic_index_in_dim(source_pts, source, 1, False),
        )
        values = lax.dynamic_index_in_dim(source_dir, source, 1, False)
        contrib = jnp.dot(
            values, kernel_block.T, precision=HIGHEST, preferred_element_type=jnp.float32
        )
        current = lax.dynamic_index_in_dim(totals, target, 1, True)
        return lax.dynamic_update_index_in_dim(totals, current + contrib[:, None, :], target, 1)

    return lax.fori_loop(start_slot, stop_slot, add_tile, partial_value)


def per_device(solution, residual, direction, noise_var, coords, tile_pairs, tile_count):
    side_count, owned_tiles, _, _, tile_size = direction.shape
    pair_count = tile_count.reshape(())
    row_ids = tile_pairs[0].reshape(-1)
    col_ids = tile_pairs[1].reshape(-1)
    squares_now = jnp.sum(residual * residual, axis=(1, 2, 3, 4))
    norm_now = lax.psum(squares_now, ("row", "col"))
    row_pts = lax.all_gather(coords, "col", axis=3, tiled=True).reshape(3, -1, tile_size)
    col_pts, col_dir = (
        lax.all_gather(coords, "row", axis=2, tiled=True),
        lax.all_gather(direction, "row", axis=2, tiled=True),
    )
    col_pts = col_pts.reshape(3, -1, tile_size)
    col_dir = col_dir.reshape(side_count, -1, tile_size)
    partial_value = jnp.zeros((side_count, row_pts.shape[1], tile_size), jnp.float32)
    partial_value = run_tiles(
        partial_value, jnp.int32(0), pair_count, row_ids, col_ids, row_pts, col_pts, col_dir
    )
    folded = lax.psum_scatter(
        partial_value.reshape(side_count, owned_tiles, 1, -1, tile_size),
        "col",
        scatter_dimension=3,
        tiled=True,
    )
    applied = noise_var[None] * direction + KERNEL_SCALE * folded
    curvature = lax.psum(jnp.sum(direction * applied, axis=(1, 2, 3, 4)), ("row", "col"))
    step_size = (norm_now / curvature)[:, None, None, None, None]
    new_solution = solution + step_size * direction
    new_residual = residual - step_size * applied
    norm_next = lax.psum(jnp.sum(new_residual * new_residual, axis=(1, 2, 3, 4)), ("row", "col"))
    beta_ratio = (norm_next / (norm_now + EPS))[:, None, None, None, None]
    new_direction = new_residual + beta_ratio * direction
    return (new_solution, new_residual, new_direction)


def solution(mesh):
    in_specs = (
        P(None, None, "row", "col", None),
        P(None, None, "row", "col", None),
        P(None, None, "row", "col", None),
        P(None, "row", "col", None),
        P(None, None, "row", "col", None),
        P(None, "row", "col", None),
        P("row", "col"),
    )
    out_specs = (
        P(None, None, "row", "col", None),
        P(None, None, "row", "col", None),
        P(None, None, "row", "col", None),
    )
    return jax.shard_map(
        per_device, mesh=mesh, in_specs=in_specs, out_specs=out_specs, check_vma=False
    )
```

profile of v0, /device:TPU:0, one launch (start us, length us, event | category | flops | bytes accessed | tf_op | source)
XLA Modules:
  0.0 572.5 jit_solution(3877492613163081918)
XLA Ops:
  7.2 0.8 copy.22
  8.0 13.9 %all_gather.11 = f32[3,8,4,1,256]{4,3,2,1,0:T(1,128)S(1)} all-gather(f32[3,8,1,1,256]{4,3,2,1,0:T(1,128)S(1)} %copy-done.3), channel_id=1, replica_groups=mesh['row'=4,'col'=8] {'row'}, dimensions={2}, use_global_device_ids=true | all-gather | bytes 122880 | tf_op jit(solution)/shard_map/all_gather | solution.py:51
  21.9 9.8 %all_gather.9 = f32[8,8,4,1,256]{4,3,2,1,0:T(1,128)S(1)} all-gather(f32[8,8,1,1,256]{4,3,2,1,0:T(1,128)S(1)} %copy-done), channel_id=1, replica_groups=mesh['row'=4,'col'=8] {'row'}, dimensions={2}, use_global_device_ids=true | all-gather | bytes 327680 | tf_op jit(solution)/shard_map/all_gather | solution.py:52
  31.7 0.7 reduce
  32.5 9.3 %all_gather.10 = f32[3,8,1,8,256]{4,1,2,0,3:T(8,128)S(1)} all-gather(f32[3,8,1,1,256]{4,1,2,0,3:T(8,128)S(1)} %copy.22), channel_id=1, replica_groups=mesh['row'=4,'col'=8] {'col'}, dimensions={3}, use_global_device_ids=true | all-gather | bytes 221184 | tf_op jit(solution)/shard_map/all_gather | solution.py:49
  42.2 127.4 %while.10 = (s32[]{:T(128)}, f32[8,64,256]{2,0,1:T(8,128)S(1)}, s32[]{:T(128)}, s32[64]{0:T(128)S(1)}, s32[64]{0:T(128)S(1)}, /*index=5*/f32[8,32,256]{2,1,0:T(8...) while((s32[]{:T(128)}, f32[8,64,256]{2,0,1:T(8,128)S(1)}, ...), condition=%wide.region_3.4_spmd, body=%wide.region_2.3_spmd.sunk | while | flops 7276557 | bytes 59699 | solution.py:39
  42.9 0.6 dynamic_slice.31
  45.4 0.6 dynamic_slice.30
  49.2 0.6 dynamic_slice.31
  51.8 0.6 dynamic_slice.30
  55.6 0.6 dynamic_slice.31
  58.1 0.6 dynamic_slice.30
  61.9 0.6 dynamic_slice.31
  64.5 0.6 dynamic_slice.30
  68.3 0.6 dynamic_slice.31
  70.8 0.6 dynamic_slice.30
  74.6 0.6 dynamic_slice.31
  77.1 0.6 dynamic_slice.30
  80.9 0.6 dynamic_slice.31
  83.5 0.6 dynamic_slice.30
  87.3 0.6 dynamic_slice.31
  89.8 0.6 dynamic_slice.30
  93.6 0.6 dynamic_slice.31
  96.2 0.6 dynamic_slice.30
  100.0 0.6 dynamic_slice.31
  102.5 0.6 dynamic_slice.30
  106.3 0.6 dynamic_slice.31
  108.8 0.6 dynamic_slice.30
  115.2 0.6 dynamic_slice.30
  121.5 0.6 dynamic_slice.30
  127.9 0.6 dynamic_slice.30
  131.7 0.6 dynamic_slice.31
  134.2 0.6 dynamic_slice.30
  140.5 0.6 dynamic_slice.30
  146.9 0.6 dynamic_slice.30
  150.7 0.6 dynamic_slice.31
  153.2 0.6 dynamic_slice.30
  159.5 0.6 dynamic_slice.30
  165.9 0.6 dynamic_slice.30
  169.7 1.1 copy.25
  170.8 0.7 copy-done.5
  171.8 310.1 %reduce-scatter.2.cloned.1.call-done = f32[8,8,1,1,256]{4,1,2,0,3:T(8,128)} async-done(((f32[8,8,1,8,256]{4,1,2,0,3:T(8,128)}), f32[8,8,1,1,256]{4,1,2,0,3:T(8,128)}) %reduce-scatter.2.cloned.1.call-update) | async-done | bytes 65552 | tf_op jit(solution)/shard_map/reduce_scatter | solution.py:60
  481.9 1.1 multiply_reduce_fusion.1
  482.9 39.4 %all-reduce = (f32[8]{0:T(128)S(1)}, f32[8]{0:T(128)S(1)}) all-reduce(f32[8]{0:T(128)S(1)} %multiply_reduce_fusion.2, f32[8]{0:T(128)S(1)} %multiply_reduce_fusion.1), channel_id=1, replica_groups=mesh['row'=4,'col'=8] {'row','col'}, use_global_device_ids=true, to_apply=%region_1.0 | all-reduce | flops 16 | bytes 128 | tf_op jit(solution)/shard_map/psum | solution.py:48
  522.5 41.0 %psum.23 = f32[8]{0:T(128)S(1)} all-reduce(f32[8]{0:T(128)S(1)} %get-tuple-element.71), channel_id=1, replica_groups=mesh['row'=4,'col'=8] {'row','col'}, use_global_device_ids=true, to_apply=%region_8.9 | all-reduce | flops 8 | bytes 64 | tf_op jit(solution)/shard_map/psum | solution.py:71
  563.5 0.7 copy.32
  564.3 0.7 copy.33
  565.0 0.7 copy.31
  (94 shorter events, 15.8 us)
Async XLA Ops:
  7.2 0.8 copy-start.3
  7.2 474.7 %reduce-scatter.2.cloned.1.call-start = ((), (), s32[]{:S(2)}) async-start(), calls=%async_computation.1 | async-start | bytes 589824 | tf_op jit(solution)/shard_map/reduce_scatter | solution.py:60
  8.0 13.9 %copy-start.6 = (s32[2,1,1,64]{3,2,1,0:T(1,128)S(1)}, s32[2,1,1,64]{3,2,1,0:T(1,128)}, u32[]{:S(2)}) copy-start(s32[2,1,1,64]{3,2,1,0:T(1,128)} %param.14) | copy-start | bytes 1540
  8.0 13.9 %copy-start = (f32[8,8,1,1,256]{4,3,2,1,0:T(1,128)S(1)}, f32[8,8,1,1,256]{4,3,2,1,0:T(1,128)}, u32[]{:S(2)}) copy-start(f32[8,8,1,1,256]{4,3,2,1,0:T(1,128)} %param.11) | copy-start | bytes 196612
  170.8 0.7 copy-start.5
  170.8 0.9 copy-start.1
  481.9 40.4 %copy-start.2 = (f32[8,8,1,1,256]{4,1,2,0,3:T(8,128)S(1)}, f32[8,8,1,1,256]{4,1,2,0,3:T(8,128)}, u32[]{:S(2)}) copy-start(f32[8,8,1,1,256]{4,1,2,0,3:T(8,128)} %reduce-scatter.2.cloned.1.call-done) | copy-start | bytes 196612
  481.9 40.4 %copy-start.4 = (f32[8,8,1,1,256]{4,3,2,1,0:T(1,128)S(1)}, f32[8,8,1,1,256]{4,3,2,1,0:T(1,128)}, u32[]{:S(2)}) copy-start(f32[8,8,1,1,256]{4,3,2,1,0:T(1,128)} %param.9) | copy-start | bytes 196612
Sparse Core Ops, SparseCore 0:
  170.9 310.8 reduce-scatter.1
where the time goes:
time: 583 us; the launch traced here: 573 us
  waiting for transfers between devices  310 us (53%)
  blocking collectives  113 us (19%)
  loops' own time  93.4 us (16%)
  local copies, waits for them, and re-layouts  29.3 us (5%)
  between operations  14.1 us (2%)
  matrix products  9.73 us (2%)
    reduce_scatter x1, waiting for transfers between devices, per_device(): lax.psum_scatter(partial_value.reshape(side_count, owned_tiles, 1, -1, ti...  310 us
    another operation x1, loops' own time, run_tiles(): return lax.fori_loop(start_slot, stop_slot, add_tile, partial_value)  93.4 us
    psum x1, blocking collectives, per_device(): lax.psum(jnp.sum(new_residual * new_residual, axis=(1, 2, 3, 4)), ('row',...  41 us
    psum x1, blocking collectives, per_device(): norm_now = lax.psum(squares_now, ('row', 'col'))  39.4 us
    all_gather x1, blocking collectives, per_device(): lax.all_gather(coords, 'row', axis=2, tiled=True)  13.9 us
    dynamic_slice x20, local copies, waits for them, and re-layouts, add_tile(): target = target_ids[pair_slot]  11.8 us
    dynamic_slice x20, local copies, waits for them, and re-layouts, add_tile(): source = source_ids[pair_slot]  11.7 us
  transfers between devices with their start and end apart: 1, of which 1 were waited for; matrix products, arithmetic and copies ran while one was open for 0% of the time, Pallas kernels for 0%

commit v1 on v0

--- a/solution.py
+++ b/solution.py
@@ -2,10 +2,12 @@
 import jax.numpy as jnp
 from jax import lax
 from jax.sharding import PartitionSpec as P
+from jax.lax import all_gather
 
 EPS = 1e-06
 KERNEL_SCALE = 0.125
 HIGHEST = lax.Precision.HIGHEST
+take_the_sizes = lambda state, named_axis: jnp.sum(all_gather(state, named_axis), 0)
 
 
 def wendland(target_pts, source_pts):
@@ -68,7 +70,9 @@
     step_size = (norm_now / curvature)[:, None, None, None, None]
     new_solution = solution + step_size * direction
     new_residual = residual - step_size * applied
-    norm_next = lax.psum(jnp.sum(new_residual * new_residual, axis=(1, 2, 3, 4)), ("row", "col"))
+    norm_next = take_the_sizes(
+        jnp.sum(new_residual * new_residual, axis=(1, 2, 3, 4)), ("row", "col")
+    )
     beta_ratio = (norm_next / (norm_now + EPS))[:, None, None, None, None]
     new_direction = new_residual + beta_ratio * direction
     return (new_solution, new_residual, new_direction)

time: 583 us -> 583 us (level)
    psum x1 -> x0, blocking collectives: 41 us -> none  [per_device(): lax.psum(jnp.sum(new_residual * new_residual, axis=(1, 2, 3, 4)), ('row',...]
    unnamed x0 -> x1, blocking collectives: none -> 41 us
where the time goes in v1:
time: 583 us; the launch traced here: 573 us
  waiting for transfers between devices  310 us (53%)
  blocking collectives  113 us (19%)
  loops' own time  93.4 us (16%)
  local copies, waits for them, and re-layouts  29.6 us (5%)
  between operations  14.1 us (2%)
  matrix products  9.73 us (2%)
    reduce_scatter x1, waiting for transfers between devices, per_device(): lax.psum_scatter(partial_value.reshape(side_count, owned_tiles, 1, -1, ti...  310 us
    another operation x1, loops' own time, run_tiles(): return lax.fori_loop(start_slot, stop_slot, add_tile, partial_value)  93.4 us
    unnamed x1, blocking collectives  41 us
    psum x1, blocking collectives, per_device(): norm_now = lax.psum(squares_now, ('row', 'col'))  39.4 us
    all_gather x1, blocking collectives, per_device(): lax.all_gather(coords, 'row', axis=2, tiled=True)  13.9 us
    dynamic_slice x20, local copies, waits for them, and re-layouts, add_tile(): target = target_ids[pair_slot]  11.8 us
    dynamic_slice x20, local copies, waits for them, and re-layouts, add_tile(): source = source_ids[pair_slot]  11.7 us
  transfers between devices with their start and end apart: 1, of which 1 were waited for; matrix products, arithmetic and copies ran while one was open for 0% of the time, Pallas kernels for 0%

profile of v1, /device:TPU:0, one launch (start us, length us, event | category | flops | bytes accessed | tf_op | source)
XLA Modules:
  0.0 572.9 jit_solution(3046663883682435765)
XLA Ops:
  7.2 0.8 copy.23
  8.0 13.9 %all_gather.17 = f32[3,8,4,1,256]{4,3,2,1,0:T(1,128)S(1)} all-gather(f32[3,8,1,1,256]{4,3,2,1,0:T(1,128)S(1)} %copy-done.3), channel_id=1, replica_groups=mesh['row'=4,'col'=8] {'row'}, dimensions={2}, use_global_device_ids=true | all-gather | bytes 122880 | tf_op jit(solution)/shard_map/all_gather | solution.py:53
  21.9 9.8 %all_gather.15 = f32[8,8,4,1,256]{4,3,2,1,0:T(1,128)S(1)} all-gather(f32[8,8,1,1,256]{4,3,2,1,0:T(1,128)S(1)} %copy-done), channel_id=1, replica_groups=mesh['row'=4,'col'=8] {'row'}, dimensions={2}, use_global_device_ids=true | all-gather | bytes 327680 | tf_op jit(solution)/shard_map/all_gather | solution.py:54
  31.7 0.7 reduce
  32.5 9.3 %all_gather.16 = f32[3,8,1,8,256]{4,1,2,0,3:T(8,128)S(1)} all-gather(f32[3,8,1,1,256]{4,1,2,0,3:T(8,128)S(1)} %copy.23), channel_id=1, replica_groups=mesh['row'=4,'col'=8] {'col'}, dimensions={3}, use_global_device_ids=true | all-gather | bytes 221184 | tf_op jit(solution)/shard_map/all_gather | solution.py:51
  42.2 127.4 %while.10 = (s32[]{:T(128)}, f32[8,64,256]{2,0,1:T(8,128)S(1)}, s32[]{:T(128)}, s32[64]{0:T(128)S(1)}, s32[64]{0:T(128)S(1)}, /*index=5*/f32[8,32,256]{2,1,0:T(8...) while((s32[]{:T(128)}, f32[8,64,256]{2,0,1:T(8,128)S(1)}, ...), condition=%wide.region_3.4_spmd, body=%wide.region_2.3_spmd.sunk | while | flops 7276557 | bytes 59699 | solution.py:41
  42.9 0.6 dynamic_slice.31
  45.4 0.6 dynamic_slice.30
  49.2 0.6 dynamic_slice.31
  51.8 0.6 dynamic_slice.30
  55.6 0.6 dynamic_slice.31
  58.1 0.6 dynamic_slice.30
  61.9 0.6 dynamic_slice.31
  64.5 0.6 dynamic_slice.30
  68.3 0.6 dynamic_slice.31
  70.8 0.6 dynamic_slice.30
  74.6 0.6 dynamic_slice.31
  77.1 0.6 dynamic_slice.30
  80.9 0.6 dynamic_slice.31
  83.5 0.6 dynamic_slice.30
  87.3 0.6 dynamic_slice.31
  89.8 0.6 dynamic_slice.30
  93.6 0.6 dynamic_slice.31
  96.2 0.6 dynamic_slice.30
  100.0 0.6 dynamic_slice.31
  102.5 0.6 dynamic_slice.30
  106.3 0.6 dynamic_slice.31
  108.8 0.6 dynamic_slice.30
  115.2 0.6 dynamic_slice.30
  121.5 0.6 dynamic_slice.30
  127.9 0.6 dynamic_slice.30
  131.7 0.6 dynamic_slice.31
  134.2 0.6 dynamic_slice.30
  140.5 0.6 dynamic_slice.30
  146.9 0.6 dynamic_slice.30
  150.7 0.6 dynamic_slice.31
  153.2 0.6 dynamic_slice.30
  159.5 0.6 dynamic_slice.30
  165.9 0.6 dynamic_slice.30
  169.7 1.1 copy.26
  170.8 0.7 copy-done.5
  171.8 310.1 %reduce-scatter.2.cloned.1.call-done = f32[8,8,1,1,256]{4,1,2,0,3:T(8,128)} async-done(((f32[8,8,1,8,256]{4,1,2,0,3:T(8,128)}), f32[8,8,1,1,256]{4,1,2,0,3:T(8,128)}) %reduce-scatter.2.cloned.1.call-update) | async-done | bytes 65552 | tf_op jit(solution)/shard_map/reduce_scatter | solution.py:62
  481.9 1.1 multiply_reduce_fusion.1
  482.9 39.4 %all-reduce.1 = (f32[8]{0:T(128)S(1)}, f32[8]{0:T(128)S(1)}) all-reduce(f32[8]{0:T(128)S(1)} %multiply_reduce_fusion.2, f32[8]{0:T(128)S(1)} %multiply_reduce_fusion.1), channel_id=1, replica_groups=mesh['row'=4,'col'=8] {'row','col'}, use_global_device_ids=true, to_apply=%region_1.0 | all-reduce | flops 16 | bytes 128 | tf_op jit(solution)/shard_map/psum | solution.py:50
  522.7 41.0 %all-reduce = f32[256]{0:T(256)S(1)} all-reduce(f32[256]{0:T(256)S(1)} %dynamic-update-slice), channel_id=2, replica_groups=mesh['row'=4,'col'=8] {'row','col'}, use_global_device_ids=true, to_apply=%add | all-reduce | flops 256 | bytes 2048
  563.8 0.7 copy.33
  564.6 0.7 copy.34
  565.3 0.7 copy.32
  (98 shorter events, 16.2 us)
Async XLA Ops:
  7.2 0.8 copy-start.3
  7.2 474.7 %reduce-scatter.2.cloned.1.call-start = ((), (), s32[]{:S(2)}) async-start(), calls=%async_computation.1 | async-start | bytes 589824 | tf_op jit(solution)/shard_map/reduce_scatter | solution.py:62
  8.0 13.9 %copy-start.6 = (s32[2,1,1,64]{3,2,1,0:T(1,128)S(1)}, s32[2,1,1,64]{3,2,1,0:T(1,128)}, u32[]{:S(2)}) copy-start(s32[2,1,1,64]{3,2,1,0:T(1,128)} %param.14) | copy-start | bytes 1540
  8.0 13.9 %copy-start = (f32[8,8,1,1,256]{4,3,2,1,0:T(1,128)S(1)}, f32[8,8,1,1,256]{4,3,2,1,0:T(1,128)}, u32[]{:S(2)}) copy-start(f32[8,8,1,1,256]{4,3,2,1,0:T(1,128)} %param.11) | copy-start | bytes 196612
  170.8 0.7 copy-start.5
  170.8 0.9 copy-start.1
  481.9 40.4 %copy-start.2 = (f32[8,8,1,1,256]{4,1,2,0,3:T(8,128)S(1)}, f32[8,8,1,1,256]{4,1,2,0,3:T(8,128)}, u32[]{:S(2)}) copy-start(f32[8,8,1,1,256]{4,1,2,0,3:T(8,128)} %reduce-scatter.2.cloned.1.call-done) | copy-start | bytes 196612
  481.9 40.4 %copy-start.4 = (f32[8,8,1,1,256]{4,3,2,1,0:T(1,128)S(1)}, f32[8,8,1,1,256]{4,3,2,1,0:T(1,128)}, u32[]{:S(2)}) copy-start(f32[8,8,1,1,256]{4,3,2,1,0:T(1,128)} %param.9) | copy-start | bytes 196612
Sparse Core Ops, SparseCore 0:
  170.9 310.8 reduce-scatter.1

commit v2 on v0

--- a/solution.py
+++ b/solution.py
@@ -68,7 +68,8 @@
     step_size = (norm_now / curvature)[:, None, None, None, None]
     new_solution = solution + step_size * direction
     new_residual = residual - step_size * applied
-    norm_next = lax.psum(jnp.sum(new_residual * new_residual, axis=(1, 2, 3, 4)), ("row", "col"))
+    partial = lax.psum(jnp.sum(new_residual * new_residual, axis=(1, 2, 3, 4)), "col")
+    norm_next = lax.psum(partial, "row")
     beta_ratio = (norm_next / (norm_now + EPS))[:, None, None, None, None]
     new_direction = new_residual + beta_ratio * direction
     return (new_solution, new_residual, new_direction)

time: 583 us -> 565 us (0.969)
  blocking collectives: 113 us -> 95.6 us
    psum x1 -> x2, blocking collectives: 41 us -> 23.3 us  [the longest x1 12.7 us: per_device(): lax.psum(jnp.sum(new_residual * new_residual, axis=(1, 2, 3, 4)), 'col')]
where the time goes in v2:
time: 565 us; the launch traced here: 555 us
  waiting for transfers between devices  310 us (55%)
  blocking collectives  95.6 us (17%)
  loops' own time  93.4 us (17%)
  local copies, waits for them, and re-layouts  29.3 us (5%)
  between operations  14.1 us (2%)
  matrix products  9.73 us (2%)
    reduce_scatter x1, waiting for transfers between devices, per_device(): lax.psum_scatter(partial_value.reshape(side_count, owned_tiles, 1, -1, ti...  310 us
    another operation x1, loops' own time, run_tiles(): return lax.fori_loop(start_slot, stop_slot, add_tile, partial_value)  93.4 us
    psum x1, blocking collectives, per_device(): norm_now = lax.psum(squares_now, ('row', 'col'))  39.4 us
    all_gather x1, blocking collectives, per_device(): lax.all_gather(coords, 'row', axis=2, tiled=True)  13.9 us
    psum x1, blocking collectives, per_device(): lax.psum(jnp.sum(new_residual * new_residual, axis=(1, 2, 3, 4)), 'col')  12.7 us
    dynamic_slice x20, local copies, waits for them, and re-layouts, add_tile(): target = target_ids[pair_slot]  11.8 us
    dynamic_slice x20, local copies, waits for them, and re-layouts, add_tile(): source = source_ids[pair_slot]  11.7 us
  transfers between devices with their start and end apart: 1, of which 1 were waited for; matrix products, arithmetic and copies ran while one was open for 0% of the time, Pallas kernels for 0%

profile of v2, /device:TPU:0, one launch (start us, length us, event | category | flops | bytes accessed | tf_op | source)
XLA Modules:
  0.0 554.8 jit_solution(7096577884687991700)
XLA Ops:
  7.2 0.8 copy.22
  8.0 13.9 %all_gather.11 = f32[3,8,4,1,256]{4,3,2,1,0:T(1,128)S(1)} all-gather(f32[3,8,1,1,256]{4,3,2,1,0:T(1,128)S(1)} %copy-done.3), channel_id=1, replica_groups=mesh['row'=4,'col'=8] {'row'}, dimensions={2}, use_global_device_ids=true | all-gather | bytes 122880 | tf_op jit(solution)/shard_map/all_gather | solution.py:51
  21.9 9.8 %all_gather.9 = f32[8,8,4,1,256]{4,3,2,1,0:T(1,128)S(1)} all-gather(f32[8,8,1,1,256]{4,3,2,1,0:T(1,128)S(1)} %copy-done), channel_id=1, replica_groups=mesh['row'=4,'col'=8] {'row'}, dimensions={2}, use_global_device_ids=true | all-gather | bytes 327680 | tf_op jit(solution)/shard_map/all_gather | solution.py:52
  31.7 0.7 reduce
  32.5 9.3 %all_gather.10 = f32[3,8,1,8,256]{4,1,2,0,3:T(8,128)S(1)} all-gather(f32[3,8,1,1,256]{4,1,2,0,3:T(8,128)S(1)} %copy.22), channel_id=1, replica_groups=mesh['row'=4,'col'=8] {'col'}, dimensions={3}, use_global_device_ids=true | all-gather | bytes 221184 | tf_op jit(solution)/shard_map/all_gather | solution.py:49
  42.2 127.4 %while.10 = (s32[]{:T(128)}, f32[8,64,256]{2,0,1:T(8,128)S(1)}, s32[]{:T(128)}, s32[64]{0:T(128)S(1)}, s32[64]{0:T(128)S(1)}, /*index=5*/f32[8,32,256]{2,1,0:T(8...) while((s32[]{:T(128)}, f32[8,64,256]{2,0,1:T(8,128)S(1)}, ...), condition=%wide.region_3.4_spmd, body=%wide.region_2.3_spmd.sunk | while | flops 7276557 | bytes 59699 | solution.py:39
  42.9 0.6 dynamic_slice.31
  45.4 0.6 dynamic_slice.30
  49.2 0.6 dynamic_slice.31
  51.8 0.6 dynamic_slice.30
  55.6 0.6 dynamic_slice.31
  58.1 0.6 dynamic_slice.30
  61.9 0.6 dynamic_slice.31
  64.5 0.6 dynamic_slice.30
  68.3 0.6 dynamic_slice.31
  70.8 0.6 dynamic_slice.30
  74.6 0.6 dynamic_slice.31
  77.1 0.6 dynamic_slice.30
  80.9 0.6 dynamic_slice.31
  83.5 0.6 dynamic_slice.30
  87.3 0.6 dynamic_slice.31
  89.8 0.6 dynamic_slice.30
  93.6 0.6 dynamic_slice.31
  96.2 0.6 dynamic_slice.30
  100.0 0.6 dynamic_slice.31
  102.5 0.6 dynamic_slice.30
  108.8 0.6 dynamic_slice.30
  115.2 0.6 dynamic_slice.30
  121.5 0.6 dynamic_slice.30
  127.9 0.6 dynamic_slice.30
  131.7 0.6 dynamic_slice.31
  134.2 0.6 dynamic_slice.30
  140.5 0.6 dynamic_slice.30
  146.9 0.6 dynamic_slice.30
  150.7 0.6 dynamic_slice.31
  153.2 0.6 dynamic_slice.30
  159.5 0.6 dynamic_slice.30
  165.9 0.6 dynamic_slice.30
  169.7 1.1 copy.25
  170.8 0.7 copy-done.5
  171.8 310.1 %reduce-scatter.2.cloned.1.call-done = f32[8,8,1,1,256]{4,1,2,0,3:T(8,128)} async-done(((f32[8,8,1,8,256]{4,1,2,0,3:T(8,128)}), f32[8,8,1,1,256]{4,1,2,0,3:T(8,128)}) %reduce-scatter.2.cloned.1.call-update) | async-done | bytes 65552 | tf_op jit(solution)/shard_map/reduce_scatter | solution.py:60
  481.9 1.1 multiply_reduce_fusion.1
  482.9 39.4 %all-reduce = (f32[8]{0:T(128)S(1)}, f32[8]{0:T(128)S(1)}) all-reduce(f32[8]{0:T(128)S(1)} %multiply_reduce_fusion.2, f32[8]{0:T(128)S(1)} %multiply_reduce_fusion.1), channel_id=1, replica_groups=mesh['row'=4,'col'=8] {'row','col'}, use_global_device_ids=true, to_apply=%region_1.0 | all-reduce | flops 16 | bytes 128 | tf_op jit(solution)/shard_map/psum | solution.py:48
  522.5 12.7 %psum.30 = f32[8]{0:T(128)S(1)} all-reduce(f32[8]{0:T(128)S(1)} %get-tuple-element.71), channel_id=1, replica_groups=mesh['row'=4,'col'=8] {'col'}, use_global_device_ids=true, to_apply=%region_8.9 | all-reduce | flops 8 | bytes 64 | tf_op jit(solution)/shard_map/psum | solution.py:71
  535.2 10.6 %psum.31 = f32[8]{0:T(128)S(1)} all-reduce(f32[8]{0:T(128)S(1)} %psum.30), channel_id=1, replica_groups=mesh['row'=4,'col'=8] {'row'}, use_global_device_ids=true, to_apply=%region_9.10 | all-reduce | flops 8 | bytes 64 | tf_op jit(solution)/shard_map/psum | solution.py:72
  545.8 0.7 copy.32
  546.5 0.7 copy.33
  547.2 0.7 copy.31
  (95 shorter events, 16.4 us)
Async XLA Ops:
  7.2 0.8 copy-start.3
  7.2 474.7 %reduce-scatter.2.cloned.1.call-start = ((), (), s32[]{:S(2)}) async-start(), calls=%async_computation.1 | async-start | bytes 589824 | tf_op jit(solution)/shard_map/reduce_scatter | solution.py:60
  8.0 13.9 %copy-start.6 = (s32[2,1,1,64]{3,2,1,0:T(1,128)S(1)}, s32[2,1,1,64]{3,2,1,0:T(1,128)}, u32[]{:S(2)}) copy-start(s32[2,1,1,64]{3,2,1,0:T(1,128)} %param.14) | copy-start | bytes 1540
  8.0 13.9 %copy-start = (f32[8,8,1,1,256]{4,3,2,1,0:T(1,128)S(1)}, f32[8,8,1,1,256]{4,3,2,1,0:T(1,128)}, u32[]{:S(2)}) copy-start(f32[8,8,1,1,256]{4,3,2,1,0:T(1,128)} %param.11) | copy-start | bytes 196612
  170.8 0.7 copy-start.5
  170.8 0.9 copy-start.1
  481.9 40.4 %copy-start.2 = (f32[8,8,1,1,256]{4,1,2,0,3:T(8,128)S(1)}, f32[8,8,1,1,256]{4,1,2,0,3:T(8,128)}, u32[]{:S(2)}) copy-start(f32[8,8,1,1,256]{4,1,2,0,3:T(8,128)} %reduce-scatter.2.cloned.1.call-done) | copy-start | bytes 196612
  481.9 40.4 %copy-start.4 = (f32[8,8,1,1,256]{4,3,2,1,0:T(1,128)S(1)}, f32[8,8,1,1,256]{4,3,2,1,0:T(1,128)}, u32[]{:S(2)}) copy-start(f32[8,8,1,1,256]{4,3,2,1,0:T(1,128)} %param.9) | copy-start | bytes 196612
Sparse Core Ops, SparseCore 0:
  170.9 310.8 reduce-scatter.1
